TPU v7x, 256 devices: a whole 4x4x8 slice. The times are simulated.
256 devices in a mesh: seq: 32 (over z, x), head: 8 (over y, core).
Axes of the slice: x: 4, y: 4, z: 8, core: 2. Of those that a mesh axis runs over, the one named last changes fastest.
Arguments:
- queries: bfloat16 [16384, 4096], P('seq', 'head'), may hold values from -0.3984375 to 0.3984375
- keys: bfloat16 [16384, 4096], P('seq', 'head'), may hold values from -0.3984375 to 0.3984375
- values: bfloat16 [16384, 1024], P('seq', 'head'), may hold values from -3 to 3
- out_grad: bfloat16 [16384, 1024], P('seq', 'head'), may hold values from -0.29882812 to 0.29882812
- transitions: bfloat16 [32, 256, 256], replicated, may hold values from -1 to 1, as said below
- gammas: float32 [16], P('head'), may hold values from 0.6 to 1
- regimes: int32 [64], replicated, may hold values from 0 to 31
- documents: int32 [64], replicated, may hold values from 0 to 7, never falling along the last dimension, each value on 1 to 32 neighbouring positions
Outputs:
- query_grad: bfloat16 [16384, 4096], P('seq', 'head')
- key_grad: bfloat16 [16384, 4096], P('seq', 'head')
- value_grad: bfloat16 [16384, 1024], P('seq', 'head')
- regime_grad: float32 [32, 256, 256], P('seq', 'head')
Inputs may be any that keep to these rules, and one draw needn't show every extreme that they name: `transitions`: diagonal entries lie in 0.9 to 1.0, the others are small. `documents`: document numbers never fall; each document spans at most 32 blocks and one spans exactly that many.
All inputs are finite; a program needn't handle non-finite values.
Results may differ from a plain program's by a relative error of at most 0.005.
Values sent between devices are 32-bit elements; how exact they have to be, the bound alone decides.
A program may use at most 64 MiB of HBM per device.

v0:
```python
import jax
import jax.numpy as jnp
from jax import lax
from jax.sharding import PartitionSpec as P

STATE = 256
HEAD_DIM = 64
REGIMES = 32
BLOCK = 256


PRECISE = lax.Precision.HIGHEST


def from_behind(x, axis, by):
    count = lax.axis_size(axis)
    pairs = [(i, i + by) for i in range(count) if 0 <= i + by < count]
    return lax.ppermute(x, axis, pairs)


def rotate(matrix, state):
    return jnp.einsum("nm,hmp->hnp", matrix, state, precision=PRECISE)


def extend_forward(current, matrix, keep_one, update, decays):
    current_mat, current_scale, current_sum = current
    factor = keep_one * decays
    return (
        keep_one * jnp.dot(matrix, current_mat, precision=PRECISE),
        decays * current_scale,
        update + factor[:, None, None] * rotate(matrix, current_sum),
    )


def extend_backward(current, matrix, keep_one, source, decays):
    current_mat, current_scale, current_sum = current
    factor = keep_one * decays
    flipped = matrix.T
    return (
        keep_one * jnp.dot(flipped, current_mat, precision=PRECISE),
        decays * current_scale,
        factor[:, None, None] * rotate(flipped, source + current_sum),
    )


def apply_map(current, state):
    current_mat, current_scale, current_sum = current
    return current_scale[:, None, None] * rotate(current_mat, state) + current_sum


def relay_forward(current):
    devices_seq = lax.axis_size("seq")

    def relay_step(number, carried_pair):
        arriving = from_behind(carried_pair[1], "seq", 1)
        return (arriving, apply_map(current, arriving))

    initial = (jnp.zeros_like(current[2]), current[2])
    return lax.fori_loop(0, devices_seq - 1, relay_step, initial)[0]


def relay_backward(current):
    devices_seq = lax.axis_size("seq")

    def relay_step(number, carried_pair):
        arriving = from_behind(carried_pair[1], "seq", -1)
        return (arriving, apply_map(current, arriving))

    initial = (jnp.zeros_like(current[2]), current[2])
    return lax.fori_loop(0, devices_seq - 1, relay_step, initial)[0]


def local(queries, keys, values, out_grad, transitions, gammas, regimes, documents):
    tokens_dev = queries.shape[0]
    heads_dev = gammas.shape[0]
    blocks_dev = tokens_dev // BLOCK
    query_rows = queries.reshape(blocks_dev, BLOCK, heads_dev, STATE)
    key_rows = keys.reshape(blocks_dev, BLOCK, heads_dev, STATE)
    value_rows = values.reshape(blocks_dev, BLOCK, heads_dev, HEAD_DIM)
    grad_rows = out_grad.reshape(blocks_dev, BLOCK, heads_dev, HEAD_DIM)
    first_block = lax.axis_index("seq") * blocks_dev
    same_doc = (documents[1:] == documents[:-1]).astype(jnp.float32)
    kept_all = jnp.concatenate([jnp.zeros((1,), jnp.float32), same_doc])
    kept = lax.dynamic_slice_in_dim(kept_all, first_block, blocks_dev)
    picked = lax.dynamic_slice_in_dim(regimes, first_block, blocks_dev)
    matrices = jnp.take(transitions, picked, axis=0).astype(jnp.float32)
    updates = jnp.einsum(
        "clhn,clhp->chnp", key_rows, value_rows, preferred_element_type=jnp.float32
    )
    sources = jnp.einsum(
        "clhn,clhp->chnp", query_rows, grad_rows, preferred_element_type=jnp.float32
    )
    eye_mat = jnp.eye(STATE, dtype=jnp.float32)
    ones_scale = jnp.ones((heads_dev,), jnp.float32)
    zero_state = jnp.zeros((heads_dev, STATE, HEAD_DIM), jnp.float32)
    identity = (eye_mat, ones_scale, zero_state)
    forward_map = identity
    for number in range(blocks_dev):
        forward_map = extend_forward(
            forward_map, matrices[number], kept[number], updates[number], gammas
        )
    backward_map = identity
    for number in reversed(range(blocks_dev)):
        backward_map = extend_backward(
            backward_map, matrices[number], kept[number], sources[number], gammas
        )
    state_in = relay_forward(forward_map)
    grad_in = relay_backward(backward_map)
    previous = state_in
    entry_list = []
    before_list = []
    for number in range(blocks_dev):
        factor = kept[number] * gammas
        entry = factor[:, None, None] * rotate(matrices[number], previous)
        before_list.append(previous)
        entry_list.append(entry)
        previous = entry + updates[number]
    carried = grad_in
    leave_list = [None] * blocks_dev
    total_list = [None] * blocks_dev
    for number in reversed(range(blocks_dev)):
        leave_list[number] = carried
        total = sources[number] + carried
        total_list[number] = total
        factor = kept[number] * gammas
        carried = factor[:, None, None] * jnp.einsum(
            "nm,hnp->hmp", matrices[number], total, precision=PRECISE
        )
    terms = jnp.stack(
        [
            kept[number]
            * jnp.einsum(
                "h,hnp,hmp->nm", gammas, total_list[number], before_list[number], precision=PRECISE
            )
            for number in range(blocks_dev)
        ]
    )
    head_summed = lax.psum_scatter(terms, "head", scatter_dimension=1, tiled=True)
    owned = REGIMES // lax.axis_size("seq")
    regime_ids = jnp.arange(owned * lax.axis_size("seq"), dtype=jnp.int32)
    onehot = (picked[:, None] == regime_ids[None, :]).astype(jnp.float32)
    regime_grad = lax.psum_scatter(
        jnp.einsum("cr,cij->rij", onehot, head_summed, precision=PRECISE),
        "seq",
        scatter_dimension=0,
        tiled=True,
    )
    entries_b = jnp.stack(entry_list).astype(jnp.bfloat16)
    leaving_b = jnp.stack(leave_list).astype(jnp.bfloat16)
    causal = lax.broadcasted_iota(jnp.int32, (BLOCK, BLOCK), 0) >= lax.broadcasted_iota(
        jnp.int32, (BLOCK, BLOCK), 1
    )

    def within(inputs):
        query_block, key_block, value_block, grad_block, entry_block, leave_block = inputs
        scores = jnp.einsum(
            "lhn,shn->hls", query_block, key_block, preferred_element_type=jnp.float32
        )
        probs = jnp.where(causal[None], scores, 0.0).astype(jnp.bfloat16)
        dots = jnp.einsum(
            "lhp,shp->hls", grad_block, value_block, preferred_element_type=jnp.float32
        )
        dscore = jnp.where(causal[None], dots, 0.0).astype(jnp.bfloat16)
        query_grad = jnp.einsum(
            "lhp,hnp->lhn", grad_block, entry_block, preferred_element_type=jnp.float32
        ) + jnp.einsum("hls,shn->lhn", dscore, key_block, preferred_element_type=jnp.float32)
        key_grad = jnp.einsum(
            "shp,hnp->shn", value_block, leave_block, preferred_element_type=jnp.float32
        ) + jnp.einsum("hls,lhn->shn", dscore, query_block, preferred_element_type=jnp.float32)
        value_grad = jnp.einsum(
            "shn,hnp->shp", key_block, leave_block, preferred_element_type=jnp.float32
        ) + jnp.einsum("hls,lhp->shp", probs, grad_block, preferred_element_type=jnp.float32)
        return (
            query_grad.astype(jnp.bfloat16),
            key_grad.astype(jnp.bfloat16),
            value_grad.astype(jnp.bfloat16),
        )

    query_grad, key_grad, value_grad = lax.map(
        within, (query_rows, key_rows, value_rows, grad_rows, entries_b, leaving_b)
    )
    return (
        query_grad.reshape(tokens_dev, heads_dev * STATE),
        key_grad.reshape(tokens_dev, heads_dev * STATE),
        value_grad.reshape(tokens_dev, heads_dev * HEAD_DIM),
        regime_grad,
    )


def solution(mesh):
    in_specs = (
        P("seq", "head"),
        P("seq", "head"),
        P("seq", "head"),
        P("seq", "head"),
        P(),
        P("head"),
        P(),
        P(),
    )
    out_specs = (P("seq", "head"), P("seq", "head"), P("seq", "head"), P("seq", "head", None))
    return jax.shard_map(local, mesh=mesh, in_specs=in_specs, out_specs=out_specs, check_vma=False)
```

profile of v0, /device:TPU:1, one launch (start us, length us, event | category | flops | bytes accessed | tf_op | source)
XLA Modules:
  0.0 966.2 jit_solution(18396770703167704760)
XLA Ops:
  21.9 263.1 %while.41 = (s32[]{:T(128)}, f32[2,256,64]{1,2,0:T(8,128)}, f32[2,256,64]{1,2,0:T(8,128)S(1)}, f32[2]{0:T(128)S(1)}, f32[256,256]{1,0:T(8,128)S(1)}, /*index=5*/f32[2,256,64]{1,2,0:T(8,128)S(1)}, s32[]{:T(128)}) while((s32[]{:T(128)}, f32[2,256,64]{1,2,0:T(8,128)}, f32[2,256,64]{1,2,0:T(8,128)S(1)}, f32[2]{0:T(128)S(1)}, ...), condition=%wide.region_3.4_spmd, body=%wide.region_2.3_spmd.sunk | while | flops 100728832 | bytes 1704089 | solution.py:70
  23.2 5.0 collective-permute-done.1
  30.1 5.0 collective-permute-done.1
  43.4 5.8 collective-permute-done.1
  51.1 6.5 collective-permute-done.1
  59.5 6.5 collective-permute-done.1
  68.0 6.5 collective-permute-done.1
  76.5 6.5 collective-permute-done.1
  84.9 7.6 collective-permute-done.1
  94.5 8.4 collective-permute-done.1
  104.8 7.2 collective-permute-done.1
  114.0 5.6 collective-permute-done.1
  121.5 6.2 collective-permute-done.1
  129.7 6.5 collective-permute-done.1
  138.1 6.5 collective-permute-done.1
  146.6 6.5 collective-permute-done.1
  155.1 6.5 collective-permute-done.1
  163.5 7.9 collective-permute-done.1
  173.4 8.5 collective-permute-done.1
  183.8 6.2 collective-permute-done.1
  192.0 6.0 collective-permute-done.1
  199.9 6.0 collective-permute-done.1
  207.8 6.5 collective-permute-done.1
  216.3 6.5 collective-permute-done.1
  224.7 6.5 collective-permute-done.1
  233.2 6.9 collective-permute-done.1
  242.1 8.3 collective-permute-done.1
  252.4 7.3 collective-permute-done.1
  261.6 6.7 collective-permute-done.1
  270.2 5.7 collective-permute-done.1
  277.9 6.5 collective-permute-done.1
  287.9 285.3 %while.40 = (s32[]{:T(128)}, f32[2,256,64]{1,2,0:T(8,128)}, f32[2,256,64]{1,2,0:T(8,128)S(1)}, f32[2]{0:T(128)S(1)}, f32[256,256]{1,0:T(8,128)S(1)}, /*index=5*/f32[2,256,64]{1,2,0:T(8,128)S(1)}, s32[]{:T(128)}) while((s32[]{:T(128)}, f32[2,256,64]{1,2,0:T(8,128)}, f32[2,256,64]{1,2,0:T(8,128)S(1)}, f32[2]{0:T(128)S(1)}, ...), condition=%wide.region_1.2_spmd, body=%wide.region_0.1_spmd.sunk | while | flops 100728832 | bytes 1704089 | solution.py:59
  287.9 5.5 collective-permute-start
  295.9 5.5 collective-permute-start
  304.0 5.5 collective-permute-start
  325.1 5.8 collective-permute-start
  333.5 6.9 collective-permute-start
  343.0 7.2 collective-permute-start
  352.8 9.4 collective-permute-start
  365.0 6.4 collective-permute-start
  374.3 6.7 collective-permute-start
  383.6 7.4 collective-permute-start
  393.6 6.6 collective-permute-start
  402.8 6.3 collective-permute-start
  411.7 6.4 collective-permute-start
  420.6 5.9 collective-permute-start
  429.2 6.2 collective-permute-start
  438.0 6.3 collective-permute-start
  448.2 6.0 collective-permute-start
  457.1 6.7 collective-permute-start
  466.4 6.2 collective-permute-start
  475.2 6.1 collective-permute-start
  483.9 6.9 collective-permute-start
  493.3 7.4 collective-permute-start
  503.3 8.4 collective-permute-start
  514.3 7.4 collective-permute-start
  524.3 7.3 collective-permute-start
  534.2 6.8 collective-permute-start
  543.6 7.2 collective-permute-start
  553.4 7.2 collective-permute-start
  563.3 6.7 collective-permute-start
  579.0 163.2 %reduce-scatter.3.cloned.1.call-done = f32[2,32,256]{2,1,0:T(8,128)} async-done(((f32[2,256,256]{2,1,0:T(8,128)}), f32[2,32,256]{2,1,0:T(8,128)}) %reduce-scatter.3.cloned.1.call-update) | async-done | bytes 65552 | tf_op jit(solution)/shard_map/reduce_scatter | solution.py:138
  745.3 8.4 while.42
  757.6 201.8 %reduce-scatter.5.cloned.1.call-done = f32[1,32,256]{2,1,0:T(8,128)} async-done(((f32[32,32,256]{2,1,0:T(8,128)}), f32[1,32,256]{2,1,0:T(8,128)}) %reduce-scatter.5.cloned.1.call-update) | async-done | bytes 32784 | tf_op jit(solution)/shard_map/reduce_scatter | solution.py:142
  (342 shorter events, 192.7 us)
Async XLA Ops:
  7.2 735.0 %reduce-scatter.3.cloned.1.call-start = ((), (), s32[]{:S(2)}) async-start(), calls=%async_computation.2 | async-start | bytes 589824 | tf_op jit(solution)/shard_map/reduce_scatter | solution.py:138
  21.9 6.3 collective-permute-start.1
  28.8 6.2 collective-permute-start.1
  35.7 5.7 collective-permute-start.1
  42.1 7.1 collective-permute-start.1
  49.8 7.8 collective-permute-start.1
  58.3 7.8 collective-permute-start.1
  66.7 7.8 collective-permute-start.1
  75.2 7.8 collective-permute-start.1
  83.7 8.9 collective-permute-start.1
  93.2 9.6 collective-permute-start.1
  103.5 8.5 collective-permute-start.1
  112.7 6.8 collective-permute-start.1
  120.2 7.5 collective-permute-start.1
  128.4 7.8 collective-permute-start.1
  136.8 7.8 collective-permute-start.1
  145.3 7.8 collective-permute-start.1
  153.8 7.8 collective-permute-start.1
  162.2 9.2 collective-permute-start.1
  172.1 9.8 %collective-permute-start.1 = (f32[2,256,64]{1,2,0:T(8,128)S(1)}, f32[2,256,64]{1,2,0:T(8,128)S(1)}, u32[]{:S(2)}, u32[]{:S(2)}) collective-permute-start(f32[2,256,64]{1,2,0:T(8,128)S(1)} %get-tuple-element.433), channel_id=1, source_target_pairs={{8,0},{16,8},{24,16},{32,24},{40,32},{48,40},{56,48},{64,56},{72,6... | collective-permute-start | bytes 393224 | tf_op jit(solution)/shard_map/while/body/eval_jaxpr/ppermute | solution.py:18
  182.5 7.5 collective-permute-start.1
  190.7 7.2 collective-permute-start.1
  198.6 7.2 collective-permute-start.1
  206.5 7.8 collective-permute-start.1
  215.0 7.8 collective-permute-start.1
  223.4 7.8 collective-permute-start.1
  231.9 8.2 collective-permute-start.1
  240.8 9.6 collective-permute-start.1
  251.1 8.6 collective-permute-start.1
  260.3 7.9 collective-permute-start.1
  268.9 7.0 collective-permute-start.1
  276.6 7.8 collective-permute-start.1
  287.9 7.4 collective-permute-start
  295.9 7.4 collective-permute-start
  304.0 7.4 collective-permute-start
  312.0 5.7 collective-permute-start
  318.4 6.0 collective-permute-start
  325.1 7.8 collective-permute-start
  333.5 8.8 collective-permute-start
  343.0 9.2 collective-permute-start
  352.8 11.6 %collective-permute-start = (f32[2,256,64]{1,2,0:T(8,128)S(1)}, f32[2,256,64]{1,2,0:T(8,128)S(1)}, u32[]{:S(2)}, u32[]{:S(2)}) collective-permute-start(f32[2,256,64]{1,2,0:T(8,128)S(1)} %get-tuple-element.412), channel_id=1, source_target_pairs={{0,8},{8,16},{16,24},{24,32},{32,40},{40,48},{48,56},{56,64},{64,7... | collective-permute-start | bytes 393224 | tf_op jit(solution)/shard_map/while/body/eval_jaxpr/ppermute | solution.py:18
  365.0 8.6 collective-permute-start
  374.3 8.7 collective-permute-start
  383.6 9.3 collective-permute-start
  393.6 8.6 collective-permute-start
  402.8 8.2 collective-permute-start
  411.7 8.3 collective-permute-start
  420.6 7.9 collective-permute-start
  429.2 8.1 collective-permute-start
  438.0 9.6 collective-permute-start
  448.2 8.2 collective-permute-start
  457.1 8.7 collective-permute-start
  466.4 8.2 collective-permute-start
  475.2 8.0 collective-permute-start
  483.9 8.8 collective-permute-start
  493.3 9.3 collective-permute-start
  503.3 10.4 %collective-permute-start = (f32[2,256,64]{1,2,0:T(8,128)S(1)}, f32[2,256,64]{1,2,0:T(8,128)S(1)}, u32[]{:S(2)}, u32[]{:S(2)}) collective-permute-start(f32[2,256,64]{1,2,0:T(8,128)S(1)} %get-tuple-element.412), channel_id=1, source_target_pairs={{0,8},{8,16},{16,24},{24,32},{32,40},{40,48},{48,56},{56,64},{64,7... | collective-permute-start | bytes 393224 | tf_op jit(solution)/shard_map/while/body/eval_jaxpr/ppermute | solution.py:18
  514.3 9.4 collective-permute-start
  524.3 9.3 collective-permute-start
  534.2 8.8 collective-permute-start
  543.6 9.1 collective-permute-start
  553.4 9.2 collective-permute-start
  563.3 9.3 collective-permute-start
  578.5 380.8 %reduce-scatter.5.cloned.1.call-start = ((), (), s32[]{:S(2)}) async-start(), calls=%async_computation.3 | async-start | bytes 1081344 | tf_op jit(solution)/shard_map/reduce_scatter | solution.py:142
  (66 other events, 899.9 us)
Sparse Core Ops, SparseCore 0:
  578.6 163.5 reduce-scatter.2
  746.6 212.7 reduce-scatter.4
where the time goes:
time: 973 us; the launch traced here: 966 us
  waiting for transfers between devices  630 us (65%)
  starting transfers between devices  242 us (25%)
  matrix products  41 us (4%)
  local copies, waits for them, and re-layouts  32.5 us (3%)
  between operations  14.4 us (1%)
    ppermute x62, waiting for transfers between devices, from_behind(): return lax.ppermute(x, axis, pairs)  265 us
    ppermute x62, starting transfers between devices, from_behind(): return lax.ppermute(x, axis, pairs)  242 us
    reduce_scatter x1, waiting for transfers between devices, local(): lax.psum_scatter(jnp.einsum('cr,cij->rij', onehot, head_summed, precision...  202 us
    reduce_scatter x1, waiting for transfers between devices, local(): lax.psum_scatter(terms, 'head', scatter_dimension=1, tiled=True)  163 us
    dot_general x68, matrix products, rotate(): return jnp.einsum('nm,hmp->hnp', matrix, state, precision=PRECISE)  27.3 us
  transfers between devices with their start and end apart: 64, of which 64 were waited for; matrix products, arithmetic and copies ran while one was open for 1% of the time, Pallas kernels for 0%

commit v1 on v0

v1 whole, which is shorter than its diff:
```python
import functools

import jax
import jax.numpy as jnp
from jax import lax
from jax.experimental import pallas as pl
from jax.experimental.pallas import tpu as pltpu
from jax.sharding import PartitionSpec as P

BLOCK = 256
STATE = 256
HEAD_DIM = 64
HEADS_DEV = 2
X = 4
CORES = 2
BACK = 4
MESH = pl.DeviceIdType.MESH
F32 = jnp.float32
BF16 = jnp.bfloat16
NN = (((1,), (0,)), ((), ()))
NT = (((1,), (1,)), ((), ()))
TN = (((0,), (0,)), ((), ()))


def dot(a, b, dims):
    return lax.dot_general(a, b, dims, preferred_element_type=F32)


def split(a):
    high = a.astype(BF16)
    return high, (a - high.astype(F32)).astype(BF16)


def turn(state, matrix, dims):
    rows = state.shape[0]
    both = dot(jnp.concatenate(split(state), axis=0), matrix, dims)
    return both[:rows] + both[rows:]


def turn_split(state, high, low, dims):
    rows = state.shape[0]
    state_high, state_low = split(state)
    both = dot(jnp.concatenate([state_high, state_low], axis=0), high, dims)
    return both[:rows] + both[rows:] + dot(state_high, low, dims)


def product(a, b):
    a_high, a_low = a
    b_high, b_low = b
    return dot(a_high, b_high, NN) + (dot(a_high, b_low, NN) + dot(a_low, b_high, NN))


def kernel(
    sizes,
    regimes,
    documents,
    gammas,
    q_hbm,
    k_hbm,
    v_hbm,
    g_hbm,
    t_hbm,
    qo_hbm,
    ko_hbm,
    vo_hbm,
    ro_hbm,
    q,
    k,
    v,
    g,
    mats,
    qo,
    ko,
    vo,
    ro,
    q_part,
    k_part,
    v_part,
    update,
    source,
    pairs,
    groups,
    inner,
    t_send,
    t_recv,
    z_send,
    z_fwd,
    z_bwd,
    s_send,
    s_recv,
    terms,
    h_core,
    h_sum,
    h_y,
    h_block,
    h_x,
    h_reg,
    h_z,
    in_sem,
    out_sem,
    send_sem,
    recv_sem,
):
    Z, Y, N, HD, B = sizes
    rows = HEADS_DEV * HD
    piece = rows // X
    seq = lax.axis_index("seq")
    head = lax.axis_index("head")
    z, x = seq // X, seq % X
    y, core = head // CORES, head % CORES

    def at(dz, dx, dy, dc):
        where = ((z + dz) % Z * X + (x + dx) % X, (y + dy) % Y * CORES + (core + dc) % CORES)
        return where

    loads = [
        pltpu.make_async_copy(src, dst, in_sem.at[i])
        for i, (src, dst) in enumerate(
            [(k_hbm, k), (v_hbm, v), (g_hbm, g), (q_hbm, q), (t_hbm, mats)]
        )
    ]
    for load in loads:
        load.start()

    peers = (
        [at(0, j, 0, 0) for j in range(1, X)]
        + [at(j, 0, 0, 0) for j in range(1, Z)]
        + [at(0, 0, j, 0) for j in range(1, Y)]
        + [at(0, 0, 0, 1)]
    )
    barrier = pltpu.get_barrier_semaphore()
    for peer in peers:
        pl.semaphore_signal(barrier, inc=1, device_id=peer, device_id_type=MESH)

    used = [0]

    def send(src, dst, peer):
        number = used[0]
        used[0] += 1
        return pltpu.make_async_remote_copy(
            src_ref=src,
            dst_ref=dst,
            send_sem=send_sem.at[number],
            recv_sem=recv_sem.at[number],
            device_id=peer,
            device_id_type=MESH,
        )

    def kept(c):
        same = documents[c] == documents[jnp.maximum(c - 1, 0)]
        return jnp.where(same, 1.0, 0.0).astype(F32) * jnp.where(c > 0, 1.0, 0.0).astype(F32)

    def matrix(c):
        return mats[regimes[c]]

    row_id = lax.broadcasted_iota(jnp.int32, (rows, 1), 0)
    gamma_rows = jnp.where(row_id < HD, gammas[0], gammas[1])
    lane_id = lax.broadcasted_iota(jnp.int32, (1, rows), 1)
    lane_mask = [lane_id < HD, lane_id >= HD]
    first = seq * 2
    keep = [kept(first), kept(first + 1)]

    def tokens(b):
        return slice(b * B, (b + 1) * B)

    def lanes(h):
        return slice(h * N, (h + 1) * N)

    loads[0].wait()
    loads[1].wait()
    for b in range(2):
        flipped = v[tokens(b), :].T
        for h in range(HEADS_DEV):
            part = slice(h * HD, (h + 1) * HD)
            update[b, part, :] = dot(flipped[part], k[tokens(b), lanes(h)], NN)
    loads[2].wait()
    loads[3].wait()
    for b in range(2):
        flipped = g[tokens(b), :].T
        for h in range(HEADS_DEV):
            part = slice(h * HD, (h + 1) * HD)
            source[b, part, :] = dot(flipped[part], q[tokens(b), lanes(h)], NN)
    loads[4].wait()
    m0 = matrix(first)
    m1 = matrix(first + 1)
    ahead = update[1] + keep[1] * gamma_rows * turn(update[0], m1, NT)
    behind = source[0] + keep[1] * gamma_rows * turn(source[1], m1, NN)
    behind = keep[0] * gamma_rows * turn(behind, m0, NN)
    for j in range(X):
        part = slice(j * piece, (j + 1) * piece)
        t_send[j, 0] = ahead[part]
        t_send[j, 1] = behind[part]

    pl.semaphore_wait(barrier, len(peers))
    first_round = [
        send(t_send.at[(x + j) % X], t_recv.at[x], at(0, j, 0, 0)) for j in range(1, X)
    ]
    for copy in first_round:
        copy.start()
    t_recv[x] = t_send[x]

    def pair_product(c):
        return dot(matrix(c + 1), matrix(c), NN)

    base = z * 2 * X
    for j in range(X):
        high, low = split(pair_product(base + 2 * j))
        pairs[j, 0] = high
        pairs[j, 1] = low

    def pair(j):
        return pairs[j, 0], pairs[j, 1]

    def group_product(number, offset):
        group = (z + offset + Z) % Z
        made = [split(pair_product(group * 2 * X + 2 * j)) for j in range(X)]
        while len(made) > 1:
            made = [split(product(made[i + 1], made[i])) for i in range(0, len(made), 2)]
        groups[number, 0] = made[0][0]
        groups[number, 1] = made[0][1]

    @pl.loop(0, BACK - 1)
    def _(i):
        group_product(i, -1 - i)

    gamma = gammas[(x * piece) // HD]
    gamma2 = gamma * gamma
    scale = [gamma2 * kept(base + 2 * j) * kept(base + 2 * j + 1) for j in range(X)]

    for copy in first_round:
        copy.wait()
    run = t_recv[0, 0]
    before = [None, run]
    for j in range(1, X):
        run = t_recv[j, 0] + scale[j] * turn_split(run, *pair(j), NT)
        before.append(run)
    run = t_recv[X - 1, 1]
    after = [None] * X
    for j in reversed(range(X - 1)):
        after[j] = run
        run = t_recv[j, 1] + scale[j] * turn_split(run, *pair(j), NN)
    z_send[0] = before[X]
    z_send[1] = run
    second_round = []
    for j in range(1, BACK + 1):
        second_round.append(send(z_send.at[0], z_fwd.at[j - 1], at(j, 0, 0, 0)))
        second_round.append(send(z_send.at[1], z_bwd.at[j - 1], at(-j + Z, 0, 0, 0)))
    for copy in second_round:
        copy.start()

    @pl.loop(0, BACK - 1)
    def _(i):
        group_product(BACK - 1 + i, 1 + i)

    made = pair(0)
    for j in range(1, X - 1):
        made = split(product(pair(j), made))
        inner[0, j - 1, 0] = made[0]
        inner[0, j - 1, 1] = made[1]
    made = pair(X - 1)
    for j in reversed(range(1, X - 1)):
        made = split(product(made, pair(j)))
        inner[1, j - 1, 0] = made[0]
        inner[1, j - 1, 1] = made[1]

    row = lax.broadcasted_iota(jnp.int32, (B, B), 0)
    column = lax.broadcasted_iota(jnp.int32, (B, B), 1)
    for b in range(2):
        for h in range(HEADS_DEV):
            q_block = q[tokens(b), lanes(h)]
            k_block = k[tokens(b), lanes(h)]
            v_block = v[tokens(b), :]
            g_block = g[tokens(b), :]
            zero = jnp.zeros_like(g_block)
            g_head = jnp.where(lane_mask[h], g_block, zero)
            probs = jnp.where(row <= column, dot(k_block, q_block, NT), 0.0).astype(BF16)
            scored = jnp.where(row >= column, dot(g_head, v_block, NT), 0.0).astype(BF16)
            turned = jnp.where(row <= column, dot(v_block, g_head, NT), 0.0).astype(BF16)
            q_part[tokens(b), lanes(h)] = dot(scored, k_block, NN)
            k_part[tokens(b), lanes(h)] = dot(turned, q_block, NN)
            if h == 0:
                v_part[tokens(b), :] = dot(probs, g_head, NN)
            else:
                v_part[tokens(b), :] += dot(probs, g_head, NN)

    gamma_group = jnp.float32(1.0)
    for j in range(X):
        gamma_group = gamma_group * gamma2

    def group_scale(offset):
        group = (z + offset + Z) % Z
        total = gamma_group
        for j in range(2 * X):
            total = total * kept(group * 2 * X + j)
        return total

    for copy in second_round:
        copy.wait()
    inbound = z_fwd[BACK - 1]
    outbound = z_bwd[BACK - 1]
    for j in reversed(range(BACK - 1)):
        inbound = z_fwd[j] + group_scale(-1 - j) * turn_split(
            inbound, groups[j, 0], groups[j, 1], NT
        )
        outbound = z_bwd[j] + group_scale(1 + j) * turn_split(
            outbound, groups[BACK - 1 + j, 0], groups[BACK - 1 + j, 1], NN
        )
    s_send[0, 0] = inbound
    total_scale = scale[0]
    for j in range(1, X):
        made = pair(0) if j == 1 else (inner[0, j - 2, 0], inner[0, j - 2, 1])
        s_send[j, 0] = before[j] + total_scale * turn_split(inbound, *made, NT)
        total_scale = total_scale * scale[j]
    s_send[X - 1, 1] = outbound
    total_scale = scale[X - 1]
    for j in reversed(range(X - 1)):
        made = pair(X - 1) if j == X - 2 else (inner[1, j, 0], inner[1, j, 1])
        s_send[j, 1] = after[j] + total_scale * turn_split(outbound, *made, NN)
        total_scale = total_scale * scale[j]
    third_round = [
        send(s_send.at[(x + j) % X], s_recv.at[x], at(0, j, 0, 0)) for j in range(1, X)
    ]
    for copy in third_round:
        copy.start()
    s_recv[x] = s_send[x]
    for copy in third_round:
        copy.wait()

    previous = jnp.concatenate([s_recv[j, 0] for j in range(X)], axis=0)
    leaving = jnp.concatenate([s_recv[j, 1] for j in range(X)], axis=0)
    total1 = source[1] + leaving
    entry0 = keep[0] * gamma_rows * turn(previous, m0, NT)
    leave0 = keep[1] * gamma_rows * turn(total1, m1, NN)
    end0 = entry0 + update[0]
    total0 = source[0] + leave0
    for b, (left, right) in enumerate([(total0, previous), (total1, end0)]):
        left_high, left_low = split(left * (keep[b] * gamma_rows))
        right_high, right_low = split(right)
        term = dot(
            jnp.concatenate([left_high, left_low, left_high], axis=0),
            jnp.concatenate([right_high, right_high, right_low], axis=0),
            TN,
        )
        height = N // (Y * CORES)
        for j in range(Y * CORES):
            terms[j % CORES, j // CORES, b] = term[j * height : (j + 1) * height]
    core_copy = send(terms.at[1 - core], h_core, at(0, 0, 0, 1))
    core_copy.start()

    entry1 = keep[1] * gamma_rows * turn(end0, m1, NT)
    entries = [entry0.astype(BF16), entry1.astype(BF16)]
    leaves = [leave0.astype(BF16), leaving.astype(BF16)]

    core_copy.wait()
    for j in range(Y):
        h_sum[j] = terms[core, j] + h_core[j]
    y_round = [send(h_sum.at[(y + j) % Y], h_y.at[j - 1], at(0, 0, j, 0)) for j in range(1, Y)]
    for copy in y_round:
        copy.start()

    stores = []
    for b in range(2):
        v_block = v[tokens(b), :]
        g_block = g[tokens(b), :]
        zero = jnp.zeros_like(g_block)
        v_new = v_part[tokens(b), :]
        for h in range(HEADS_DEV):
            g_head = jnp.where(lane_mask[h], g_block, zero)
            v_head = jnp.where(lane_mask[h], v_block, zero)
            qo[tokens(b), lanes(h)] = (
                q_part[tokens(b), lanes(h)] + dot(g_head, entries[b], NN)
            ).astype(BF16)
            ko[tokens(b), lanes(h)] = (
                k_part[tokens(b), lanes(h)] + dot(v_head, leaves[b], NN)
            ).astype(BF16)
            v_new = v_new + jnp.where(
                lane_mask[h], dot(k[tokens(b), lanes(h)], leaves[b], NT), 0.0
            )
        vo[tokens(b), :] = v_new.astype(BF16)
    for i, (src, dst) in enumerate([(qo, qo_hbm), (ko, ko_hbm), (vo, vo_hbm)]):
        stores.append(pltpu.make_async_copy(src, dst, out_sem.at[i]))
        stores[-1].start()

    for copy in y_round:
        copy.wait()
    mine = h_sum[y]
    for j in range(Y - 1):
        mine = mine + h_y[j]
    h_block[...] = mine
    x_round = [send(h_block, h_x.at[x], at(0, j, 0, 0)) for j in range(1, X)]
    for copy in x_round:
        copy.start()
    h_x[x] = mine
    for copy in x_round:
        copy.wait()
    for j in range(Z):
        owner = (z + j) % Z * X + x
        total = jnp.zeros_like(ro[...])
        for i in range(2 * X):
            chosen = jnp.where(regimes[base + i] == owner, 1.0, 0.0).astype(F32)
            total = total + chosen * h_x[i // 2, i % 2]
        h_reg[j] = total
    z_round = [send(h_reg.at[j], h_z.at[j - 1], at(j, 0, 0, 0)) for j in range(1, Z)]
    for copy in z_round:
        copy.start()
    for copy in z_round:
        copy.wait()
    final = h_reg[0]
    for j in range(Z - 1):
        final = final + h_z[j]
    ro[...] = final
    last = pltpu.make_async_copy(ro, ro_hbm.at[0], out_sem.at[3])
    last.start()
    for store in stores:
        store.wait()
    last.wait()


def local(Z, Y, queries, keys, values, out_grad, transitions, gammas, regimes, documents):
    tokens_dev = queries.shape[0]
    N = transitions.shape[1]
    rows = values.shape[1]
    HD = rows // HEADS_DEV
    B = tokens_dev // 2
    piece = rows // X
    height = N // (Y * CORES)
    anywhere = pl.BlockSpec(memory_space=pl.ANY)
    scalar = pl.BlockSpec(memory_space=pltpu.SMEM)
    vmem = pltpu.VMEM
    copies = 3 * (X - 1) + 2 * BACK + 1 + (Y - 1) + (Z - 1)
    return pl.pallas_call(
        functools.partial(kernel, (Z, Y, N, HD, B)),
        out_shape=(
            jax.ShapeDtypeStruct(queries.shape, BF16),
            jax.ShapeDtypeStruct(keys.shape, BF16),
            jax.ShapeDtypeStruct(values.shape, BF16),
            jax.ShapeDtypeStruct((1, height, N), F32),
        ),
        in_specs=[scalar] * 3 + [anywhere] * 5,
        out_specs=[anywhere] * 4,
        scratch_shapes=[
            vmem(queries.shape, BF16),
            vmem(keys.shape, BF16),
            vmem(values.shape, BF16),
            vmem(values.shape, BF16),
            vmem(transitions.shape, BF16),
            vmem(queries.shape, BF16),
            vmem(keys.shape, BF16),
            vmem(values.shape, BF16),
            vmem((height, N), F32),
            vmem(queries.shape, F32),
            vmem(keys.shape, F32),
            vmem(values.shape, F32),
            vmem((2, rows, N), F32),
            vmem((2, rows, N), F32),
            vmem((X, 2, N, N), BF16),
            vmem((2 * (BACK - 1), 2, N, N), BF16),
            vmem((2, X - 2, 2, N, N), BF16),
            vmem((X, 2, piece, N), F32),
            vmem((X, 2, piece, N), F32),
            vmem((2, piece, N), F32),
            vmem((BACK, piece, N), F32),
            vmem((BACK, piece, N), F32),
            vmem((X, 2, piece, N), F32),
            vmem((X, 2, piece, N), F32),
            vmem((CORES, Y, 2, height, N), F32),
            vmem((Y, 2, height, N), F32),
            vmem((Y, 2, height, N), F32),
            vmem((Y - 1, 2, height, N), F32),
            vmem((2, height, N), F32),
            vmem((X, 2, height, N), F32),
            vmem((Z, height, N), F32),
            vmem((Z - 1, height, N), F32),
            pltpu.SemaphoreType.DMA((5,)),
            pltpu.SemaphoreType.DMA((4,)),
            pltpu.SemaphoreType.DMA((copies,)),
            pltpu.SemaphoreType.DMA((copies,)),
        ],
        compiler_params=pltpu.CompilerParams(collective_id=0, has_side_effects=True),
        name="whole",
    )(regimes, documents, gammas, queries, keys, values, out_grad, transitions)


def solution(mesh):
    in_specs = (
        P("seq", "head"),
        P("seq", "head"),
        P("seq", "head"),
        P("seq", "head"),
        P(),
        P("head"),
        P(),
        P(),
    )
    out_specs = (P("seq", "head"), P("seq", "head"), P("seq", "head"), P("seq", "head", None))
    body = functools.partial(local, mesh.shape["seq"] // X, mesh.shape["head"] // CORES)
    return jax.shard_map(body, mesh=mesh, in_specs=in_specs, out_specs=out_specs, check_vma=False)
```

time: 973 us -> 60.5 us (0.06)
  waiting for transfers between devices: 630 us -> 0 us
  starting transfers between devices: 242 us -> 0 us
  Pallas kernels: 0 us -> 52.8 us
  matrix products: 41 us -> 0 us
  local copies, waits for them, and re-layouts: 32.5 us -> 6.68 us
  between operations: 14.4 us -> 0.64 us
    reduce_scatter x2 -> x0, waiting for transfers between devices: 365 us -> none  [the longest x1 202 us: local(): lax.psum_scatter(jnp.einsum('cr,cij->rij', onehot, head_summed, precision...]
    ppermute x62 -> x0, waiting for transfers between devices: 265 us -> none  [from_behind(): return lax.ppermute(x, axis, pairs)]
    ppermute x62 -> x0, starting transfers between devices: 242 us -> none  [from_behind(): return lax.ppermute(x, axis, pairs)]
    pallas_call x0 -> x1, Pallas kernels: none -> 52.8 us  [local(): pl.pallas_call(functools.partial(kernel, (Z, Y, N, HD, B)), out_shape=(ja...]
    dot_general x92 -> x0, matrix products: 41 us -> none  [the longest x68 27.3 us: rotate(): return jnp.einsum('nm,hmp->hnp', matrix, state, precision=PRECISE)]
    while x124 -> x0, local copies, waits for them, and re-layouts: 15.4 us -> none
  transfers between devices with their start and end apart: 64 -> 0, of which waited for: 64 -> 0; matrix products, arithmetic and copies ran while one was open for 1% -> 0% of each run, Pallas kernels for 0% -> 0%
where the time goes in v1:
time: 60.5 us; the launch traced here: 60.2 us
  Pallas kernels  52.8 us (87%)
  local copies, waits for them, and re-layouts  6.68 us (11%)
  between operations  0.64 us (1%)
    pallas_call x1, Pallas kernels, local(): pl.pallas_call(functools.partial(kernel, (Z, Y, N, HD, B)), out_shape=(ja...  52.8 us
    unnamed x4, local copies, waits for them, and re-layouts  6.68 us

profile of v1, /device:TPU:1, one launch (start us, length us, event | category | flops | bytes accessed | tf_op | source)
XLA Modules:
  0.0 60.2 jit_solution(17392838440687894844)
XLA Ops:
  0.6 52.8 %whole.1 = (bf16[512,512]{1,0:T(8,128)(2,1)}, bf16[512,512]{1,0:T(8,128)(2,1)}, bf16[512,128]{1,0:T(8,128)(2,1)}, f32[1,32,256]{2,1,0:T(8,128)}) custom-call(s32[64]{0:T(128)} %regimes.1, s32[64]{0:T(128)} %documents.1, f32[2]{0:T(128)} %gammas.1, bf16[512,512]{1,0:T(8,128)(2,1)} %q_hbm.1, bf16[512,512]{1,0:T(8,128)(2,1)} %k_hbm.1, bf16[512,128]{1,0:T(8,128)(2,1)} %v_hbm.1, ...), custom_call_target="tpu_custom_call" | custom-call | tf_op jit(solution)/shard_map/whole/pallas_call | solution.py:431
  53.5 1.9 %copy.16 = bf16[512,512]{1,0:T(8,128)(2,1)} copy(bf16[512,512]{1,0:T(8,128)(2,1)} %get-tuple-element.8) | data formatting | bytes 1048576
  55.4 1.9 %copy.17 = bf16[512,512]{1,0:T(8,128)(2,1)} copy(bf16[512,512]{1,0:T(8,128)(2,1)} %get-tuple-element.9) | data formatting | bytes 1048576
  57.2 1.6 %copy.18 = bf16[512,128]{1,0:T(8,128)(2,1)} copy(bf16[512,128]{1,0:T(8,128)(2,1)} %get-tuple-element.10) | data formatting | bytes 262144
  58.8 1.4 %copy.19 = f32[1,32,256]{2,1,0:T(8,128)} copy(f32[1,32,256]{2,1,0:T(8,128)} %get-tuple-element.11) | data formatting | bytes 65536

commit v2 on v1

--- a/solution.py
+++ b/solution.py
@@ -14,6 +14,7 @@
 X = 4
 CORES = 2
 BACK = 4
+PARTS = 2
 MESH = pl.DeviceIdType.MESH
 F32 = jnp.float32
 BF16 = jnp.bfloat16
@@ -60,19 +61,15 @@
     v_hbm,
     g_hbm,
     t_hbm,
-    qo_hbm,
-    ko_hbm,
-    vo_hbm,
-    ro_hbm,
+    qo,
+    ko,
+    vo,
+    ro,
     q,
     k,
     v,
     g,
     mats,
-    qo,
-    ko,
-    vo,
-    ro,
     q_part,
     k_part,
     v_part,
@@ -97,7 +94,6 @@
     h_reg,
     h_z,
     in_sem,
-    out_sem,
     send_sem,
     recv_sem,
 ):
@@ -342,23 +338,65 @@
             TN,
         )
         height = N // (Y * CORES)
+        width = N // PARTS
         for j in range(Y * CORES):
-            terms[j % CORES, j // CORES, b] = term[j * height : (j + 1) * height]
-    core_copy = send(terms.at[1 - core], h_core, at(0, 0, 0, 1))
-    core_copy.start()
+            for t in range(PARTS):
+                terms[t, j % CORES, j // CORES, b] = term[
+                    j * height : (j + 1) * height, t * width : (t + 1) * width
+                ]
+    core_round = [send(terms.at[t, 1 - core], h_core.at[t], at(0, 0, 0, 1)) for t in range(PARTS)]
+    for copy in core_round:
+        copy.start()
 
     entry1 = keep[1] * gamma_rows * turn(end0, m1, NT)
     entries = [entry0.astype(BF16), entry1.astype(BF16)]
     leaves = [leave0.astype(BF16), leaving.astype(BF16)]
 
-    core_copy.wait()
-    for j in range(Y):
-        h_sum[j] = terms[core, j] + h_core[j]
-    y_round = [send(h_sum.at[(y + j) % Y], h_y.at[j - 1], at(0, 0, j, 0)) for j in range(1, Y)]
-    for copy in y_round:
-        copy.start()
-
-    stores = []
+    y_round = []
+    for t in range(PARTS):
+        core_round[t].wait()
+        for j in range(Y):
+            h_sum[t, j] = terms[t, core, j] + h_core[t, j]
+        copies = [
+            send(h_sum.at[t, (y + j) % Y], h_y.at[t, j - 1], at(0, 0, j, 0)) for j in range(1, Y)
+        ]
+        for copy in copies:
+            copy.start()
+        y_round.append(copies)
+    x_round = []
+    for t in range(PARTS):
+        for copy in y_round[t]:
+            copy.wait()
+        mine = h_sum[t, y]
+        for j in range(Y - 1):
+            mine = mine + h_y[t, j]
+        h_block[t] = mine
+        copies = [send(h_block.at[t], h_x.at[t, x], at(0, j, 0, 0)) for j in range(1, X)]
+        for copy in copies:
+            copy.start()
+        x_round.append(copies)
+        h_x[t, x] = mine
+    chosen = [
+        [
+            jnp.where(regimes[base + i] == (z + j) % Z * X + x, 1.0, 0.0).astype(F32)
+            for i in range(2 * X)
+        ]
+        for j in range(Z)
+    ]
+    z_round = []
+    for t in range(PARTS):
+        for copy in x_round[t]:
+            copy.wait()
+        for j in range(Z):
+            total = chosen[j][0] * h_x[t, 0, 0]
+            for i in range(1, 2 * X):
+                total = total + chosen[j][i] * h_x[t, i // 2, i % 2]
+            h_reg[t, j] = total
+        copies = [send(h_reg.at[t, j], h_z.at[t, j - 1], at(j, 0, 0, 0)) for j in range(1, Z)]
+        for copy in copies:
+            copy.start()
+        z_round.append(copies)
+
     for b in range(2):
         v_block = v[tokens(b), :]
         g_block = g[tokens(b), :]
@@ -377,43 +415,24 @@
                 lane_mask[h], dot(k[tokens(b), lanes(h)], leaves[b], NT), 0.0
             )
         vo[tokens(b), :] = v_new.astype(BF16)
-    for i, (src, dst) in enumerate([(qo, qo_hbm), (ko, ko_hbm), (vo, vo_hbm)]):
-        stores.append(pltpu.make_async_copy(src, dst, out_sem.at[i]))
-        stores[-1].start()
-
-    for copy in y_round:
+
+    for t in range(PARTS):
+        for copy in z_round[t]:
+            copy.wait()
+        total = h_reg[t, 0]
+        for j in range(Z - 1):
+            total = total + h_z[t, j]
+        ro[0, :, t * width : (t + 1) * width] = total
+
+
+def write(*refs):
+    count = (len(refs) - 1) // 2
+    sem = refs[-1]
+    copies = [pltpu.make_async_copy(refs[i], refs[count + i], sem.at[i]) for i in range(count)]
+    for copy in copies:
+        copy.start()
+    for copy in copies:
         copy.wait()
-    mine = h_sum[y]
-    for j in range(Y - 1):
-        mine = mine + h_y[j]
-    h_block[...] = mine
-    x_round = [send(h_block, h_x.at[x], at(0, j, 0, 0)) for j in range(1, X)]
-    for copy in x_round:
-        copy.start()
-    h_x[x] = mine
-    for copy in x_round:
-        copy.wait()
-    for j in range(Z):
-        owner = (z + j) % Z * X + x
-        total = jnp.zeros_like(ro[...])
-        for i in range(2 * X):
-            chosen = jnp.where(regimes[base + i] == owner, 1.0, 0.0).astype(F32)
-            total = total + chosen * h_x[i // 2, i % 2]
-        h_reg[j] = total
-    z_round = [send(h_reg.at[j], h_z.at[j - 1], at(j, 0, 0, 0)) for j in range(1, Z)]
-    for copy in z_round:
-        copy.start()
-    for copy in z_round:
-        copy.wait()
-    final = h_reg[0]
-    for j in range(Z - 1):
-        final = final + h_z[j]
-    ro[...] = final
-    last = pltpu.make_async_copy(ro, ro_hbm.at[0], out_sem.at[3])
-    last.start()
-    for store in stores:
-        store.wait()
-    last.wait()
 
 
 def local(Z, Y, queries, keys, values, out_grad, transitions, gammas, regimes, documents):
@@ -427,27 +446,24 @@
     anywhere = pl.BlockSpec(memory_space=pl.ANY)
     scalar = pl.BlockSpec(memory_space=pltpu.SMEM)
     vmem = pltpu.VMEM
-    copies = 3 * (X - 1) + 2 * BACK + 1 + (Y - 1) + (Z - 1)
-    return pl.pallas_call(
+    width = N // PARTS
+    copies = 2 * (X - 1) + 2 * BACK + PARTS * (1 + (Y - 1) + (X - 1) + (Z - 1))
+    results = pl.pallas_call(
         functools.partial(kernel, (Z, Y, N, HD, B)),
         out_shape=(
-            jax.ShapeDtypeStruct(queries.shape, BF16),
-            jax.ShapeDtypeStruct(keys.shape, BF16),
-            jax.ShapeDtypeStruct(values.shape, BF16),
-            jax.ShapeDtypeStruct((1, height, N), F32),
+            vmem(queries.shape, BF16),
+            vmem(keys.shape, BF16),
+            vmem(values.shape, BF16),
+            vmem((1, height, N), F32),
         ),
         in_specs=[scalar] * 3 + [anywhere] * 5,
-        out_specs=[anywhere] * 4,
+        out_specs=[pl.BlockSpec(memory_space=vmem)] * 4,
         scratch_shapes=[
             vmem(queries.shape, BF16),
             vmem(keys.shape, BF16),
             vmem(values.shape, BF16),
             vmem(values.shape, BF16),
             vmem(transitions.shape, BF16),
-            vmem(queries.shape, BF16),
-            vmem(keys.shape, BF16),
-            vmem(values.shape, BF16),
-            vmem((height, N), F32),
             vmem(queries.shape, F32),
             vmem(keys.shape, F32),
             vmem(values.shape, F32),
@@ -463,22 +479,30 @@
             vmem((BACK, piece, N), F32),
             vmem((X, 2, piece, N), F32),
             vmem((X, 2, piece, N), F32),
-            vmem((CORES, Y, 2, height, N), F32),
-            vmem((Y, 2, height, N), F32),
-            vmem((Y, 2, height, N), F32),
-            vmem((Y - 1, 2, height, N), F32),
-            vmem((2, height, N), F32),
-            vmem((X, 2, height, N), F32),
-            vmem((Z, height, N), F32),
-            vmem((Z - 1, height, N), F32),
+            vmem((PARTS, CORES, Y, 2, height, width), F32),
+            vmem((PARTS, Y, 2, height, width), F32),
+            vmem((PARTS, Y, 2, height, width), F32),
+            vmem((PARTS, Y - 1, 2, height, width), F32),
+            vmem((PARTS, 2, height, width), F32),
+            vmem((PARTS, X, 2, height, width), F32),
+            vmem((PARTS, Z, height, width), F32),
+            vmem((PARTS, Z - 1, height, width), F32),
             pltpu.SemaphoreType.DMA((5,)),
-            pltpu.SemaphoreType.DMA((4,)),
             pltpu.SemaphoreType.DMA((copies,)),
             pltpu.SemaphoreType.DMA((copies,)),
         ],
         compiler_params=pltpu.CompilerParams(collective_id=0, has_side_effects=True),
         name="whole",
     )(regimes, documents, gammas, queries, keys, values, out_grad, transitions)
+    return pl.pallas_call(
+        write,
+        out_shape=[jax.ShapeDtypeStruct(result.shape, result.dtype) for result in results],
+        in_specs=[anywhere] * 4,
+        out_specs=[anywhere] * 4,
+        scratch_shapes=[pltpu.SemaphoreType.DMA((4,))],
+        compiler_params=pltpu.CompilerParams(vmem_limit_bytes=1 << 20),
+        name="write",
+    )(*results)
 
 
 def solution(mesh):

time: 60.5 us -> 52.2 us (0.86)
  local copies, waits for them, and re-layouts: 6.68 us -> 0 us
  Pallas kernels: 52.8 us -> 51.4 us
    unnamed x4 -> x0, local copies, waits for them, and re-layouts: 6.68 us -> none
    pallas_call x1 -> x2, Pallas kernels: 52.8 us -> 51.4 us  [the longest x1 50.4 us: local(): pl.pallas_call(functools.partial(kernel, (Z, Y, N, HD, B)), out_shape=(vm...]
where the time goes in v2:
time: 52.2 us; the launch traced here: 52 us
  Pallas kernels  51.4 us (98%)
  between operations  0.64 us (1%)
    pallas_call x1, Pallas kernels, local(): pl.pallas_call(functools.partial(kernel, (Z, Y, N, HD, B)), out_shape=(vm...  50.4 us

profile of v2, /device:TPU:1, one launch (start us, length us, event | category | flops | bytes accessed | tf_op | source)
XLA Modules:
  0.0 52.0 jit_solution(13753799965576542396)
XLA Ops:
  0.6 50.4 %whole.1 = (bf16[512,512]{1,0:T(8,128)(2,1)S(1)}, bf16[512,512]{1,0:T(8,128)(2,1)S(1)}, bf16[512,128]{1,0:T(8,128)(2,1)S(1)}, f32[1,32,256]{2,1,0:T(8,128)S(1)}) custom-call(s32[64]{0:T(128)} %regimes.1, s32[64]{0:T(128)} %documents.1, f32[2]{0:T(128)} %gammas.1, bf16[512,512]{1,0:T(8,128)(2,1)} %q_hbm.1, bf16[512,512]{1,0:T(8,128)(2,1)} %k_hbm.1, ...), custom_call_target="tpu_custom_call" | custom-call | tf_op jit(solution)/shard_map/whole/pallas_call | solution.py:451
  51.0 1.0 %write.1 = (bf16[512,512]{1,0:T(8,128)(2,1)}, bf16[512,512]{1,0:T(8,128)(2,1)}, bf16[512,128]{1,0:T(8,128)(2,1)}, f32[1,32,256]{2,1,0:T(8,128)}) custom-call(bf16[512,512]{1,0:T(8,128)(2,1)S(1)} %get-tuple-element.8.refs_0_, bf16[512,512]{1,0:T(8,128)(2,1)S(1)} %get-tuple-element.9.refs_1_, bf16[512,128]{1,0:T(8,128)(2,1)S(1)} %get-tuple-element.10.refs_2_, ...), custom_call_target="tpu_custom_call" | custom-call | tf_op jit(solution)/shard_map/write/pallas_call | solution.py:497

commit v3 on v2

--- a/solution.py
+++ b/solution.py
@@ -13,14 +13,18 @@
 HEADS_DEV = 2
 X = 4
 CORES = 2
-BACK = 4
-PARTS = 2
+PARTS = 4
+CHUNKS = 2
 MESH = pl.DeviceIdType.MESH
 F32 = jnp.float32
 BF16 = jnp.bfloat16
 NN = (((1,), (0,)), ((), ()))
 NT = (((1,), (1,)), ((), ()))
 TN = (((0,), (0,)), ((), ()))
+
+
+def far_first(count):
+    return sorted(range(1, count), key=lambda j: -min(j, count - j))
 
 
 def dot(a, b, dims):
@@ -81,6 +85,7 @@
     t_send,
     t_recv,
     z_send,
+    z_pair,
     z_fwd,
     z_bwd,
     s_send,
@@ -92,7 +97,11 @@
     h_block,
     h_x,
     h_reg,
+    h_a,
+    h_b,
     h_z,
+    up_sem,
+    down_sem,
     in_sem,
     send_sem,
     recv_sem,
@@ -100,6 +109,9 @@
     Z, Y, N, HD, B = sizes
     rows = HEADS_DEV * HD
     piece = rows // X
+    chunk = piece // CHUNKS
+    height = N // (Y * CORES)
+    part_rows, width = height // 2, N // 2
     seq = lax.axis_index("seq")
     head = lax.axis_index("head")
     z, x = seq // X, seq % X
@@ -120,7 +132,7 @@
 
     peers = (
         [at(0, j, 0, 0) for j in range(1, X)]
-        + [at(j, 0, 0, 0) for j in range(1, Z)]
+        + [at(1, 0, 0, 0), at(Z - 1, 0, 0, 0)]
         + [at(0, 0, j, 0) for j in range(1, Y)]
         + [at(0, 0, 0, 1)]
     )
@@ -183,17 +195,30 @@
     behind = source[0] + keep[1] * gamma_rows * turn(source[1], m1, NN)
     behind = keep[0] * gamma_rows * turn(behind, m0, NN)
     for j in range(X):
-        part = slice(j * piece, (j + 1) * piece)
-        t_send[j, 0] = ahead[part]
-        t_send[j, 1] = behind[part]
+        for c in range(CHUNKS):
+            part = slice(j * piece + c * chunk, j * piece + (c + 1) * chunk)
+            t_send[c, j, 0] = ahead[part]
+            t_send[c, j, 1] = behind[part]
 
     pl.semaphore_wait(barrier, len(peers))
     first_round = [
-        send(t_send.at[(x + j) % X], t_recv.at[x], at(0, j, 0, 0)) for j in range(1, X)
+        [send(t_send.at[c, (x + j) % X], t_recv.at[c, x], at(0, j, 0, 0)) for j in far_first(X)]
+        for c in range(CHUNKS)
     ]
-    for copy in first_round:
-        copy.start()
-    t_recv[x] = t_send[x]
+    for c in range(CHUNKS):
+        for copy in first_round[c]:
+            copy.start()
+        t_recv[c, x] = t_send[c, x]
+
+    def pass_on():
+        pl.semaphore_signal(up_sem, inc=1, device_id=at(1, 0, 0, 0), device_id_type=MESH)
+        pl.semaphore_signal(down_sem, inc=1, device_id=at(Z - 1, 0, 0, 0), device_id_type=MESH)
+
+    def hear():
+        pl.semaphore_wait(up_sem, 1)
+        pl.semaphore_wait(down_sem, 1)
+
+    pass_on()
 
     def pair_product(c):
         return dot(matrix(c + 1), matrix(c), NN)
@@ -207,57 +232,120 @@
     def pair(j):
         return pairs[j, 0], pairs[j, 1]
 
-    def group_product(number, offset):
+    def group_product(offset):
         group = (z + offset + Z) % Z
         made = [split(pair_product(group * 2 * X + 2 * j)) for j in range(X)]
         while len(made) > 1:
             made = [split(product(made[i + 1], made[i])) for i in range(0, len(made), 2)]
-        groups[number, 0] = made[0][0]
-        groups[number, 1] = made[0][1]
-
-    @pl.loop(0, BACK - 1)
-    def _(i):
-        group_product(i, -1 - i)
+        return made[0]
+
+    made = pair(0)
+    for j in range(1, X):
+        made = split(product(pair(j), made))
+        inner[0, j - 1, 0] = made[0]
+        inner[0, j - 1, 1] = made[1]
+    hear()
+    pass_on()
 
     gamma = gammas[(x * piece) // HD]
     gamma2 = gamma * gamma
     scale = [gamma2 * kept(base + 2 * j) * kept(base + 2 * j + 1) for j in range(X)]
 
-    for copy in first_round:
-        copy.wait()
-    run = t_recv[0, 0]
-    before = [None, run]
-    for j in range(1, X):
-        run = t_recv[j, 0] + scale[j] * turn_split(run, *pair(j), NT)
-        before.append(run)
-    run = t_recv[X - 1, 1]
-    after = [None] * X
-    for j in reversed(range(X - 1)):
-        after[j] = run
-        run = t_recv[j, 1] + scale[j] * turn_split(run, *pair(j), NN)
-    z_send[0] = before[X]
-    z_send[1] = run
-    second_round = []
-    for j in range(1, BACK + 1):
-        second_round.append(send(z_send.at[0], z_fwd.at[j - 1], at(j, 0, 0, 0)))
-        second_round.append(send(z_send.at[1], z_bwd.at[j - 1], at(-j + Z, 0, 0, 0)))
-    for copy in second_round:
-        copy.start()
-
-    @pl.loop(0, BACK - 1)
-    def _(i):
-        group_product(BACK - 1 + i, 1 + i)
-
-    made = pair(0)
-    for j in range(1, X - 1):
-        made = split(product(pair(j), made))
-        inner[0, j - 1, 0] = made[0]
-        inner[0, j - 1, 1] = made[1]
+    gamma_group = jnp.float32(1.0)
+    for j in range(X):
+        gamma_group = gamma_group * gamma2
+
+    def group_scale(offset):
+        group = (z + offset + Z) % Z
+        total = gamma_group
+        for j in range(2 * X):
+            total = total * kept(group * 2 * X + j)
+        return total
+
+    own = inner[0, X - 2, 0], inner[0, X - 2, 1]
+    own_scale = group_scale(0)
+    before, after, near, second_round = [], [], [], []
+    for c in range(CHUNKS):
+        for copy in first_round[c]:
+            copy.wait()
+        run = t_recv[c, 0, 0]
+        run_back = t_recv[c, X - 1, 1]
+        fore, back = [None, run], [None] * X
+        for j in range(1, X):
+            run = t_recv[c, j, 0] + scale[j] * turn_split(run, *pair(j), NT)
+            fore.append(run)
+            i = X - 1 - j
+            back[i] = run_back
+            run_back = t_recv[c, i, 1] + scale[i] * turn_split(run_back, *pair(i), NN)
+        before.append(fore)
+        after.append(back)
+        z_send[c, 0] = run
+        z_send[c, 1] = run_back
+        near.append(
+            [
+                send(z_send.at[c, 0], z_fwd.at[c, 0], at(1, 0, 0, 0)),
+                send(z_send.at[c, 1], z_bwd.at[c, 0], at(Z - 1, 0, 0, 0)),
+            ]
+        )
+        for copy in near[c]:
+            copy.start()
+    hear()
+    for c in range(CHUNKS):
+        for copy in near[c]:
+            copy.wait()
+        z_pair[c, 0] = z_send[c, 0] + own_scale * turn_split(z_fwd[c, 0], *own, NT)
+        z_pair[c, 1] = z_send[c, 1] + own_scale * turn_split(z_bwd[c, 0], *own, NN)
+        second_round.append(
+            [
+                send(z_pair.at[c, 0], z_fwd.at[c, 2], at(3, 0, 0, 0)),
+                send(z_pair.at[c, 1], z_bwd.at[c, 2], at(Z - 3, 0, 0, 0)),
+                send(z_pair.at[c, 0], z_fwd.at[c, 1], at(1, 0, 0, 0)),
+                send(z_pair.at[c, 1], z_bwd.at[c, 1], at(Z - 1, 0, 0, 0)),
+            ]
+        )
+        for copy in second_round[c]:
+            copy.start()
+
     made = pair(X - 1)
     for j in reversed(range(1, X - 1)):
         made = split(product(made, pair(j)))
         inner[1, j - 1, 0] = made[0]
         inner[1, j - 1, 1] = made[1]
+    back = [group_product(-1), group_product(-2)]
+    front = [group_product(1), group_product(2)]
+    for i, made in enumerate([product(back[0], back[1]), product(front[1], front[0])]):
+        groups[i, 0], groups[i, 1] = split(made)
+
+    back_scale = group_scale(-1) * group_scale(-2)
+    front_scale = group_scale(1) * group_scale(2)
+    third_round = []
+    for c in range(CHUNKS):
+        for copy in second_round[c]:
+            copy.wait()
+        inbound = z_fwd[c, 1] + back_scale * turn_split(
+            z_fwd[c, 2], groups[0, 0], groups[0, 1], NT
+        )
+        outbound = z_bwd[c, 1] + front_scale * turn_split(
+            z_bwd[c, 2], groups[1, 0], groups[1, 1], NN
+        )
+        s_send[c, 0, 0] = inbound
+        total_scale = scale[0]
+        for j in range(1, X):
+            made = pair(0) if j == 1 else (inner[0, j - 2, 0], inner[0, j - 2, 1])
+            s_send[c, j, 0] = before[c][j] + total_scale * turn_split(inbound, *made, NT)
+            total_scale = total_scale * scale[j]
+        s_send[c, X - 1, 1] = outbound
+        total_scale = scale[X - 1]
+        for j in reversed(range(X - 1)):
+            made = pair(X - 1) if j == X - 2 else (inner[1, j, 0], inner[1, j, 1])
+            s_send[c, j, 1] = after[c][j] + total_scale * turn_split(outbound, *made, NN)
+            total_scale = total_scale * scale[j]
+        third_round.append(
+            [send(s_send.at[c, (x + j) % X], s_recv.at[c, x], at(0, j, 0, 0)) for j in far_first(X)]
+        )
+        for copy in third_round[c]:
+            copy.start()
+        s_recv[c, x] = s_send[c, x]
 
     row = lax.broadcasted_iota(jnp.int32, (B, B), 0)
     column = lax.broadcasted_iota(jnp.int32, (B, B), 1)
@@ -279,70 +367,31 @@
             else:
                 v_part[tokens(b), :] += dot(probs, g_head, NN)
 
-    gamma_group = jnp.float32(1.0)
-    for j in range(X):
-        gamma_group = gamma_group * gamma2
-
-    def group_scale(offset):
-        group = (z + offset + Z) % Z
-        total = gamma_group
-        for j in range(2 * X):
-            total = total * kept(group * 2 * X + j)
-        return total
-
-    for copy in second_round:
-        copy.wait()
-    inbound = z_fwd[BACK - 1]
-    outbound = z_bwd[BACK - 1]
-    for j in reversed(range(BACK - 1)):
-        inbound = z_fwd[j] + group_scale(-1 - j) * turn_split(
-            inbound, groups[j, 0], groups[j, 1], NT
-        )
-        outbound = z_bwd[j] + group_scale(1 + j) * turn_split(
-            outbound, groups[BACK - 1 + j, 0], groups[BACK - 1 + j, 1], NN
-        )
-    s_send[0, 0] = inbound
-    total_scale = scale[0]
-    for j in range(1, X):
-        made = pair(0) if j == 1 else (inner[0, j - 2, 0], inner[0, j - 2, 1])
-        s_send[j, 0] = before[j] + total_scale * turn_split(inbound, *made, NT)
-        total_scale = total_scale * scale[j]
-    s_send[X - 1, 1] = outbound
-    total_scale = scale[X - 1]
-    for j in reversed(range(X - 1)):
-        made = pair(X - 1) if j == X - 2 else (inner[1, j, 0], inner[1, j, 1])
-        s_send[j, 1] = after[j] + total_scale * turn_split(outbound, *made, NN)
-        total_scale = total_scale * scale[j]
-    third_round = [
-        send(s_send.at[(x + j) % X], s_recv.at[x], at(0, j, 0, 0)) for j in range(1, X)
-    ]
-    for copy in third_round:
-        copy.start()
-    s_recv[x] = s_send[x]
-    for copy in third_round:
-        copy.wait()
-
-    previous = jnp.concatenate([s_recv[j, 0] for j in range(X)], axis=0)
-    leaving = jnp.concatenate([s_recv[j, 1] for j in range(X)], axis=0)
+    for copies in third_round:
+        for copy in copies:
+            copy.wait()
+
+    order = [(c, j) for j in range(X) for c in range(CHUNKS)]
+    previous = jnp.concatenate([s_recv[c, j, 0] for c, j in order], axis=0)
+    leaving = jnp.concatenate([s_recv[c, j, 1] for c, j in order], axis=0)
     total1 = source[1] + leaving
     entry0 = keep[0] * gamma_rows * turn(previous, m0, NT)
     leave0 = keep[1] * gamma_rows * turn(total1, m1, NN)
     end0 = entry0 + update[0]
     total0 = source[0] + leave0
-    for b, (left, right) in enumerate([(total0, previous), (total1, end0)]):
-        left_high, left_low = split(left * (keep[b] * gamma_rows))
-        right_high, right_low = split(right)
+    for b, (outer, inside) in enumerate([(total0, previous), (total1, end0)]):
+        left_high, left_low = split(outer * (keep[b] * gamma_rows))
+        right_high, right_low = split(inside)
         term = dot(
             jnp.concatenate([left_high, left_low, left_high], axis=0),
             jnp.concatenate([right_high, right_high, right_low], axis=0),
             TN,
         )
-        height = N // (Y * CORES)
-        width = N // PARTS
         for j in range(Y * CORES):
             for t in range(PARTS):
+                top, left = j * height + t % 2 * part_rows, t // 2 * width
                 terms[t, j % CORES, j // CORES, b] = term[
-                    j * height : (j + 1) * height, t * width : (t + 1) * width
+                    top : top + part_rows, left : left + width
                 ]
     core_round = [send(terms.at[t, 1 - core], h_core.at[t], at(0, 0, 0, 1)) for t in range(PARTS)]
     for copy in core_round:
@@ -358,7 +407,7 @@
         for j in range(Y):
             h_sum[t, j] = terms[t, core, j] + h_core[t, j]
         copies = [
-            send(h_sum.at[t, (y + j) % Y], h_y.at[t, j - 1], at(0, 0, j, 0)) for j in range(1, Y)
+            send(h_sum.at[t, (y + j) % Y], h_y.at[t, j - 1], at(0, 0, j, 0)) for j in far_first(Y)
         ]
         for copy in copies:
             copy.start()
@@ -371,7 +420,7 @@
         for j in range(Y - 1):
             mine = mine + h_y[t, j]
         h_block[t] = mine
-        copies = [send(h_block.at[t], h_x.at[t, x], at(0, j, 0, 0)) for j in range(1, X)]
+        copies = [send(h_block.at[t], h_x.at[t, x], at(0, j, 0, 0)) for j in far_first(X)]
         for copy in copies:
             copy.start()
         x_round.append(copies)
@@ -383,6 +432,7 @@
         ]
         for j in range(Z)
     ]
+    a_round = []
     z_round = []
     for t in range(PARTS):
         for copy in x_round[t]:
@@ -392,10 +442,38 @@
             for i in range(1, 2 * X):
                 total = total + chosen[j][i] * h_x[t, i // 2, i % 2]
             h_reg[t, j] = total
-        copies = [send(h_reg.at[t, j], h_z.at[t, j - 1], at(j, 0, 0, 0)) for j in range(1, Z)]
+        half = 2 if t % 2 == 0 else Z - 2
+        first_leg = [
+            send(h_reg.at[t, 4], h_a.at[t, 0], at(half, 0, 0, 0)),
+            send(h_reg.at[t, 3], h_a.at[t, 1], at(1, 0, 0, 0)),
+            send(h_reg.at[t, Z - 3], h_a.at[t, 2], at(Z - 1, 0, 0, 0)),
+        ]
+        next_leg = [
+            send(h_reg.at[t, 1], h_z.at[t, 0], at(1, 0, 0, 0)),
+            send(h_reg.at[t, Z - 1], h_z.at[t, 1], at(Z - 1, 0, 0, 0)),
+        ]
+        for copy in first_leg + next_leg:
+            copy.start()
+        a_round.append(first_leg)
+        z_round.append(next_leg)
+    for t in range(PARTS):
+        for copy in a_round[t]:
+            copy.wait()
+        ahead2 = h_reg[t, 2] + h_a[t, 1]
+        behind2 = h_reg[t, Z - 2] + h_a[t, 2]
+        if t % 2 == 0:
+            ahead2 = ahead2 + h_a[t, 0]
+        else:
+            behind2 = behind2 + h_a[t, 0]
+        h_b[t, 0] = ahead2
+        h_b[t, 1] = behind2
+        copies = [
+            send(h_b.at[t, 0], h_z.at[t, 2], at(2, 0, 0, 0)),
+            send(h_b.at[t, 1], h_z.at[t, 3], at(Z - 2, 0, 0, 0)),
+        ]
         for copy in copies:
             copy.start()
-        z_round.append(copies)
+        z_round[t] += copies
 
     for b in range(2):
         v_block = v[tokens(b), :]
@@ -420,9 +498,10 @@
         for copy in z_round[t]:
             copy.wait()
         total = h_reg[t, 0]
-        for j in range(Z - 1):
+        for j in range(4):
             total = total + h_z[t, j]
-        ro[0, :, t * width : (t + 1) * width] = total
+        top, left = t % 2 * part_rows, t // 2 * width
+        ro[0, top : top + part_rows, left : left + width] = total
 
 
 def write(*refs):
@@ -441,13 +520,13 @@
     rows = values.shape[1]
     HD = rows // HEADS_DEV
     B = tokens_dev // 2
-    piece = rows // X
+    chunk = rows // X // CHUNKS
     height = N // (Y * CORES)
     anywhere = pl.BlockSpec(memory_space=pl.ANY)
     scalar = pl.BlockSpec(memory_space=pltpu.SMEM)
     vmem = pltpu.VMEM
-    width = N // PARTS
-    copies = 2 * (X - 1) + 2 * BACK + PARTS * (1 + (Y - 1) + (X - 1) + (Z - 1))
+    part_rows, width = height // 2, N // 2
+    copies = CHUNKS * (2 * (X - 1) + 6) + PARTS * (1 + (Y - 1) + (X - 1) + 7)
     results = pl.pallas_call(
         functools.partial(kernel, (Z, Y, N, HD, B)),
         out_shape=(
@@ -470,23 +549,28 @@
             vmem((2, rows, N), F32),
             vmem((2, rows, N), F32),
             vmem((X, 2, N, N), BF16),
-            vmem((2 * (BACK - 1), 2, N, N), BF16),
-            vmem((2, X - 2, 2, N, N), BF16),
-            vmem((X, 2, piece, N), F32),
-            vmem((X, 2, piece, N), F32),
-            vmem((2, piece, N), F32),
-            vmem((BACK, piece, N), F32),
-            vmem((BACK, piece, N), F32),
-            vmem((X, 2, piece, N), F32),
-            vmem((X, 2, piece, N), F32),
-            vmem((PARTS, CORES, Y, 2, height, width), F32),
-            vmem((PARTS, Y, 2, height, width), F32),
-            vmem((PARTS, Y, 2, height, width), F32),
-            vmem((PARTS, Y - 1, 2, height, width), F32),
-            vmem((PARTS, 2, height, width), F32),
-            vmem((PARTS, X, 2, height, width), F32),
-            vmem((PARTS, Z, height, width), F32),
-            vmem((PARTS, Z - 1, height, width), F32),
+            vmem((2, 2, N, N), BF16),
+            vmem((2, X - 1, 2, N, N), BF16),
+            vmem((CHUNKS, X, 2, chunk, N), F32),
+            vmem((CHUNKS, X, 2, chunk, N), F32),
+            vmem((CHUNKS, 2, chunk, N), F32),
+            vmem((CHUNKS, 2, chunk, N), F32),
+            vmem((CHUNKS, 3, chunk, N), F32),
+            vmem((CHUNKS, 3, chunk, N), F32),
+            vmem((CHUNKS, X, 2, chunk, N), F32),
+            vmem((CHUNKS, X, 2, chunk, N), F32),
+            vmem((PARTS, CORES, Y, 2, part_rows, width), F32),
+            vmem((PARTS, Y, 2, part_rows, width), F32),
+            vmem((PARTS, Y, 2, part_rows, width), F32),
+            vmem((PARTS, Y - 1, 2, part_rows, width), F32),
+            vmem((PARTS, 2, part_rows, width), F32),
+            vmem((PARTS, X, 2, part_rows, width), F32),
+            vmem((PARTS, Z, part_rows, width), F32),
+            vmem((PARTS, 3, part_rows, width), F32),
+            vmem((PARTS, 2, part_rows, width), F32),
+            vmem((PARTS, 4, part_rows, width), F32),
+            pltpu.SemaphoreType.REGULAR,
+            pltpu.SemaphoreType.REGULAR,
             pltpu.SemaphoreType.DMA((5,)),
             pltpu.SemaphoreType.DMA((copies,)),
             pltpu.SemaphoreType.DMA((copies,)),

time: 52.2 us -> 48.8 us (0.935)
  Pallas kernels: 51.4 us -> 47.6 us
    pallas_call x1, Pallas kernels: 50.4 us -> 46.5 us  [local(): pl.pallas_call(functools.partial(kernel, (Z, Y, N, HD, B)), out_shape=(vm...]
where the time goes in v3:
time: 48.8 us; the launch traced here: 48.2 us
  Pallas kernels  47.6 us (98%)
  between operations  0.64 us (1%)
    pallas_call x1, Pallas kernels, local(): pl.pallas_call(functools.partial(kernel, (Z, Y, N, HD, B)), out_shape=(vm...  46.5 us
    pallas_call x1, Pallas kernels, local(): pl.pallas_call(write, out_shape=[jax.ShapeDtypeStruct(result.shape, resul...  1.04 us

profile of v3, /device:TPU:1, one launch (start us, length us, event | category | flops | bytes accessed | tf_op | source)
XLA Modules:
  0.0 48.2 jit_solution(680764252691796909)
XLA Ops:
  0.6 46.5 %whole.1 = (bf16[512,512]{1,0:T(8,128)(2,1)S(1)}, bf16[512,512]{1,0:T(8,128)(2,1)S(1)}, bf16[512,128]{1,0:T(8,128)(2,1)S(1)}, f32[1,32,256]{2,1,0:T(8,128)S(1)}) custom-call(s32[64]{0:T(128)} %regimes.1, s32[64]{0:T(128)} %documents.1, f32[2]{0:T(128)} %gammas.1, bf16[512,512]{1,0:T(8,128)(2,1)} %q_hbm.1, bf16[512,512]{1,0:T(8,128)(2,1)} %k_hbm.1, ...), custom_call_target="tpu_custom_call" | custom-call | tf_op jit(solution)/shard_map/whole/pallas_call | solution.py:530
  47.2 1.0 %write.1 = (bf16[512,512]{1,0:T(8,128)(2,1)}, bf16[512,512]{1,0:T(8,128)(2,1)}, bf16[512,128]{1,0:T(8,128)(2,1)}, f32[1,32,256]{2,1,0:T(8,128)}) custom-call(bf16[512,512]{1,0:T(8,128)(2,1)S(1)} %get-tuple-element.8.refs_0_, bf16[512,512]{1,0:T(8,128)(2,1)S(1)} %get-tuple-element.9.refs_1_, bf16[512,128]{1,0:T(8,128)(2,1)S(1)} %get-tuple-element.10.refs_2_, ...), custom_call_target="tpu_custom_call" | custom-call | tf_op jit(solution)/shard_map/write/pallas_call | solution.py:581

commit v4 on v3

--- a/solution.py
+++ b/solution.py
@@ -57,9 +57,9 @@
 
 def kernel(
     sizes,
-    regimes,
-    documents,
-    gammas,
+    regimes_hbm,
+    documents_hbm,
+    gammas_hbm,
     q_hbm,
     k_hbm,
     v_hbm,
@@ -69,6 +69,9 @@
     ko,
     vo,
     ro,
+    regimes,
+    documents,
+    gammas,
     q,
     k,
     v,
@@ -97,8 +100,6 @@
     h_block,
     h_x,
     h_reg,
-    h_a,
-    h_b,
     h_z,
     up_sem,
     down_sem,
@@ -124,7 +125,16 @@
     loads = [
         pltpu.make_async_copy(src, dst, in_sem.at[i])
         for i, (src, dst) in enumerate(
-            [(k_hbm, k), (v_hbm, v), (g_hbm, g), (q_hbm, q), (t_hbm, mats)]
+            [
+                (k_hbm, k),
+                (v_hbm, v),
+                (g_hbm, g),
+                (q_hbm, q),
+                (t_hbm, mats),
+                (gammas_hbm, gammas),
+                (regimes_hbm, regimes),
+                (documents_hbm, documents),
+            ]
         )
     ]
     for load in loads:
@@ -161,12 +171,9 @@
     def matrix(c):
         return mats[regimes[c]]
 
-    row_id = lax.broadcasted_iota(jnp.int32, (rows, 1), 0)
-    gamma_rows = jnp.where(row_id < HD, gammas[0], gammas[1])
     lane_id = lax.broadcasted_iota(jnp.int32, (1, rows), 1)
     lane_mask = [lane_id < HD, lane_id >= HD]
     first = seq * 2
-    keep = [kept(first), kept(first + 1)]
 
     def tokens(b):
         return slice(b * B, (b + 1) * B)
@@ -188,7 +195,11 @@
         for h in range(HEADS_DEV):
             part = slice(h * HD, (h + 1) * HD)
             source[b, part, :] = dot(flipped[part], q[tokens(b), lanes(h)], NN)
-    loads[4].wait()
+    for load in loads[4:]:
+        load.wait()
+    row_id = lax.broadcasted_iota(jnp.int32, (rows, 1), 0)
+    gamma_rows = jnp.where(row_id < HD, gammas[0], gammas[1])
+    keep = [kept(first), kept(first + 1)]
     m0 = matrix(first)
     m1 = matrix(first + 1)
     ahead = update[1] + keep[1] * gamma_rows * turn(update[0], m1, NT)
@@ -290,6 +301,7 @@
         for copy in near[c]:
             copy.start()
     hear()
+    pass_on()
     for c in range(CHUNKS):
         for copy in near[c]:
             copy.wait()
@@ -432,7 +444,7 @@
         ]
         for j in range(Z)
     ]
-    a_round = []
+    hear()
     z_round = []
     for t in range(PARTS):
         for copy in x_round[t]:
@@ -442,38 +454,12 @@
             for i in range(1, 2 * X):
                 total = total + chosen[j][i] * h_x[t, i // 2, i % 2]
             h_reg[t, j] = total
-        half = 2 if t % 2 == 0 else Z - 2
-        first_leg = [
-            send(h_reg.at[t, 4], h_a.at[t, 0], at(half, 0, 0, 0)),
-            send(h_reg.at[t, 3], h_a.at[t, 1], at(1, 0, 0, 0)),
-            send(h_reg.at[t, Z - 3], h_a.at[t, 2], at(Z - 1, 0, 0, 0)),
-        ]
-        next_leg = [
-            send(h_reg.at[t, 1], h_z.at[t, 0], at(1, 0, 0, 0)),
-            send(h_reg.at[t, Z - 1], h_z.at[t, 1], at(Z - 1, 0, 0, 0)),
-        ]
-        for copy in first_leg + next_leg:
-            copy.start()
-        a_round.append(first_leg)
-        z_round.append(next_leg)
-    for t in range(PARTS):
-        for copy in a_round[t]:
-            copy.wait()
-        ahead2 = h_reg[t, 2] + h_a[t, 1]
-        behind2 = h_reg[t, Z - 2] + h_a[t, 2]
-        if t % 2 == 0:
-            ahead2 = ahead2 + h_a[t, 0]
-        else:
-            behind2 = behind2 + h_a[t, 0]
-        h_b[t, 0] = ahead2
-        h_b[t, 1] = behind2
         copies = [
-            send(h_b.at[t, 0], h_z.at[t, 2], at(2, 0, 0, 0)),
-            send(h_b.at[t, 1], h_z.at[t, 3], at(Z - 2, 0, 0, 0)),
+            send(h_reg.at[t, j], h_z.at[t, j - 1], at(j, 0, 0, 0)) for j in far_first(Z)
         ]
         for copy in copies:
             copy.start()
-        z_round[t] += copies
+        z_round.append(copies)
 
     for b in range(2):
         v_block = v[tokens(b), :]
@@ -498,7 +484,7 @@
         for copy in z_round[t]:
             copy.wait()
         total = h_reg[t, 0]
-        for j in range(4):
+        for j in range(Z - 1):
             total = total + h_z[t, j]
         top, left = t % 2 * part_rows, t // 2 * width
         ro[0, top : top + part_rows, left : left + width] = total
@@ -523,7 +509,6 @@
     chunk = rows // X // CHUNKS
     height = N // (Y * CORES)
     anywhere = pl.BlockSpec(memory_space=pl.ANY)
-    scalar = pl.BlockSpec(memory_space=pltpu.SMEM)
     vmem = pltpu.VMEM
     part_rows, width = height // 2, N // 2
     copies = CHUNKS * (2 * (X - 1) + 6) + PARTS * (1 + (Y - 1) + (X - 1) + 7)
@@ -535,9 +520,12 @@
             vmem(values.shape, BF16),
             vmem((1, height, N), F32),
         ),
-        in_specs=[scalar] * 3 + [anywhere] * 5,
+        in_specs=[anywhere] * 8,
         out_specs=[pl.BlockSpec(memory_space=vmem)] * 4,
         scratch_shapes=[
+            pltpu.SMEM(regimes.shape, jnp.int32),
+            pltpu.SMEM(documents.shape, jnp.int32),
+            pltpu.SMEM(gammas.shape, F32),
             vmem(queries.shape, BF16),
             vmem(keys.shape, BF16),
             vmem(values.shape, BF16),
@@ -566,12 +554,10 @@
             vmem((PARTS, 2, part_rows, width), F32),
             vmem((PARTS, X, 2, part_rows, width), F32),
             vmem((PARTS, Z, part_rows, width), F32),
-            vmem((PARTS, 3, part_rows, width), F32),
-            vmem((PARTS, 2, part_rows, width), F32),
-            vmem((PARTS, 4, part_rows, width), F32),
+            vmem((PARTS, Z - 1, part_rows, width), F32),
             pltpu.SemaphoreType.REGULAR,
             pltpu.SemaphoreType.REGULAR,
-            pltpu.SemaphoreType.DMA((5,)),
+            pltpu.SemaphoreType.DMA((8,)),
             pltpu.SemaphoreType.DMA((copies,)),
             pltpu.SemaphoreType.DMA((copies,)),
         ],

time: 48.8 us -> 47.2 us (0.967)
  Pallas kernels: 47.6 us -> 46 us
    pallas_call x1, Pallas kernels: 46.5 us -> 44.9 us  [local(): pl.pallas_call(functools.partial(kernel, (Z, Y, N, HD, B)), out_shape=(vm...]
where the time goes in v4:
time: 47.2 us; the launch traced here: 46.6 us
  Pallas kernels  46 us (97%)
  between operations  0.64 us (1%)
    pallas_call x1, Pallas kernels, local(): pl.pallas_call(functools.partial(kernel, (Z, Y, N, HD, B)), out_shape=(vm...  44.9 us
    pallas_call x1, Pallas kernels, local(): pl.pallas_call(write, out_shape=[jax.ShapeDtypeStruct(result.shape, resul...  1.04 us

profile of v4, /device:TPU:1, one launch (start us, length us, event | category | flops | bytes accessed | tf_op | source)
XLA Modules:
  0.0 46.6 jit_solution(13048530967886353652)
XLA Ops:
  0.6 44.9 %whole.1 = (bf16[512,512]{1,0:T(8,128)(2,1)S(1)}, bf16[512,512]{1,0:T(8,128)(2,1)S(1)}, bf16[512,128]{1,0:T(8,128)(2,1)S(1)}, f32[1,32,256]{2,1,0:T(8,128)S(1)}) custom-call(s32[64]{0:T(128)} %regimes_hbm.1, s32[64]{0:T(128)} %documents_hbm.1, f32[2]{0:T(128)} %gammas_hbm.1, bf16[512,512]{1,0:T(8,128)(2,1)} %q_hbm.1, bf16[512,512]{1,0:T(8,128)(2,1)} %k_hbm.1, ...), custom_call_target="tpu_custom_call" | custom-call | tf_op jit(solution)/shard_map/whole/pallas_call | solution.py:515
  45.6 1.0 %write.1 = (bf16[512,512]{1,0:T(8,128)(2,1)}, bf16[512,512]{1,0:T(8,128)(2,1)}, bf16[512,128]{1,0:T(8,128)(2,1)}, f32[1,32,256]{2,1,0:T(8,128)}) custom-call(bf16[512,512]{1,0:T(8,128)(2,1)S(1)} %get-tuple-element.8.refs_0_, bf16[512,512]{1,0:T(8,128)(2,1)S(1)} %get-tuple-element.9.refs_1_, bf16[512,128]{1,0:T(8,128)(2,1)S(1)} %get-tuple-element.10.refs_2_, ...), custom_call_target="tpu_custom_call" | custom-call | tf_op jit(solution)/shard_map/write/pallas_call | solution.py:567

commit v5 on v4

--- a/solution.py
+++ b/solution.py
@@ -255,6 +255,18 @@
         made = split(product(pair(j), made))
         inner[0, j - 1, 0] = made[0]
         inner[0, j - 1, 1] = made[1]
+    made = pair(X - 1)
+    for j in reversed(range(1, X - 1)):
+        made = split(product(made, pair(j)))
+        inner[1, j - 1, 0] = made[0]
+        inner[1, j - 1, 1] = made[1]
+
+    def up_to(j):
+        return pair(0) if j == 1 else (inner[0, j - 2, 0], inner[0, j - 2, 1])
+
+    def down_to(j):
+        return pair(X - 1) if j == X - 2 else (inner[1, j, 0], inner[1, j, 1])
+
     hear()
     pass_on()
 
@@ -275,21 +287,20 @@
 
     own = inner[0, X - 2, 0], inner[0, X - 2, 1]
     own_scale = group_scale(0)
-    before, after, near, second_round = [], [], [], []
+    near, second_round = [], []
     for c in range(CHUNKS):
         for copy in first_round[c]:
             copy.wait()
-        run = t_recv[c, 0, 0]
-        run_back = t_recv[c, X - 1, 1]
-        fore, back = [None, run], [None] * X
+        run = t_recv[c, X - 1, 0]
+        factor = scale[X - 1]
+        for j in reversed(range(X - 1)):
+            run = run + factor * turn_split(t_recv[c, j, 0], *down_to(j), NT)
+            factor = factor * scale[j]
+        run_back = t_recv[c, 0, 1]
+        factor = scale[0]
         for j in range(1, X):
-            run = t_recv[c, j, 0] + scale[j] * turn_split(run, *pair(j), NT)
-            fore.append(run)
-            i = X - 1 - j
-            back[i] = run_back
-            run_back = t_recv[c, i, 1] + scale[i] * turn_split(run_back, *pair(i), NN)
-        before.append(fore)
-        after.append(back)
+            run_back = run_back + factor * turn_split(t_recv[c, j, 1], *up_to(j), NN)
+            factor = factor * scale[j]
         z_send[c, 0] = run
         z_send[c, 1] = run_back
         near.append(
@@ -318,11 +329,20 @@
         for copy in second_round[c]:
             copy.start()
 
-    made = pair(X - 1)
-    for j in reversed(range(1, X - 1)):
-        made = split(product(made, pair(j)))
-        inner[1, j - 1, 0] = made[0]
-        inner[1, j - 1, 1] = made[1]
+    before, after = [], []
+    for c in range(CHUNKS):
+        run = t_recv[c, 0, 0]
+        run_back = t_recv[c, X - 1, 1]
+        fore, back = [None, run], [None] * X
+        back[X - 2] = run_back
+        for j in range(1, X - 1):
+            run = t_recv[c, j, 0] + scale[j] * turn_split(run, *pair(j), NT)
+            fore.append(run)
+            i = X - 1 - j
+            run_back = t_recv[c, i, 1] + scale[i] * turn_split(run_back, *pair(i), NN)
+            back[i - 1] = run_back
+        before.append(fore)
+        after.append(back)
     back = [group_product(-1), group_product(-2)]
     front = [group_product(1), group_product(2)]
     for i, made in enumerate([product(back[0], back[1]), product(front[1], front[0])]):
@@ -343,14 +363,12 @@
         s_send[c, 0, 0] = inbound
         total_scale = scale[0]
         for j in range(1, X):
-            made = pair(0) if j == 1 else (inner[0, j - 2, 0], inner[0, j - 2, 1])
-            s_send[c, j, 0] = before[c][j] + total_scale * turn_split(inbound, *made, NT)
+            s_send[c, j, 0] = before[c][j] + total_scale * turn_split(inbound, *up_to(j), NT)
             total_scale = total_scale * scale[j]
         s_send[c, X - 1, 1] = outbound
         total_scale = scale[X - 1]
         for j in reversed(range(X - 1)):
-            made = pair(X - 1) if j == X - 2 else (inner[1, j, 0], inner[1, j, 1])
-            s_send[c, j, 1] = after[c][j] + total_scale * turn_split(outbound, *made, NN)
+            s_send[c, j, 1] = after[c][j] + total_scale * turn_split(outbound, *down_to(j), NN)
             total_scale = total_scale * scale[j]
         third_round.append(
             [send(s_send.at[c, (x + j) % X], s_recv.at[c, x], at(0, j, 0, 0)) for j in far_first(X)]
@@ -493,7 +511,13 @@
 def write(*refs):
     count = (len(refs) - 1) // 2
     sem = refs[-1]
-    copies = [pltpu.make_async_copy(refs[i], refs[count + i], sem.at[i]) for i in range(count)]
+    copies = []
+    for i in range(count):
+        whole = refs[i].shape[0]
+        size = whole // 2 if whole > 1 else whole
+        for start in range(0, whole, size):
+            part = pl.ds(start, size)
+            copies.append(pltpu.make_async_copy(refs[i].at[part], refs[count + i].at[part], sem.at[len(copies)]))
     for copy in copies:
         copy.start()
     for copy in copies:
@@ -569,7 +593,7 @@
         out_shape=[jax.ShapeDtypeStruct(result.shape, result.dtype) for result in results],
         in_specs=[anywhere] * 4,
         out_specs=[anywhere] * 4,
-        scratch_shapes=[pltpu.SemaphoreType.DMA((4,))],
+        scratch_shapes=[pltpu.SemaphoreType.DMA((7,))],
         compiler_params=pltpu.CompilerParams(vmem_limit_bytes=1 << 20),
         name="write",
     )(*results)

time: 47.2 us -> 47 us (level)
  no operation moved by 1% of the time
where the time goes in v5:
time: 47 us; the launch traced here: 46.3 us
  Pallas kernels  45.6 us (97%)
  between operations  0.64 us (1%)
    pallas_call x1, Pallas kernels, local(): pl.pallas_call(functools.partial(kernel, (Z, Y, N, HD, B)), out_shape=(vm...  44.6 us
    pallas_call x1, Pallas kernels, local(): pl.pallas_call(write, out_shape=[jax.ShapeDtypeStruct(result.shape, resul...  1.07 us

profile of v5, /device:TPU:1, one launch (start us, length us, event | category | flops | bytes accessed | tf_op | source)
XLA Modules:
  0.0 46.3 jit_solution(13677986202313659532)
XLA Ops:
  0.6 44.6 %whole.1 = (bf16[512,512]{1,0:T(8,128)(2,1)S(1)}, bf16[512,512]{1,0:T(8,128)(2,1)S(1)}, bf16[512,128]{1,0:T(8,128)(2,1)S(1)}, f32[1,32,256]{2,1,0:T(8,128)S(1)}) custom-call(s32[64]{0:T(128)} %regimes_hbm.1, s32[64]{0:T(128)} %documents_hbm.1, f32[2]{0:T(128)} %gammas_hbm.1, bf16[512,512]{1,0:T(8,128)(2,1)} %q_hbm.1, bf16[512,512]{1,0:T(8,128)(2,1)} %k_hbm.1, ...), custom_call_target="tpu_custom_call" | custom-call | tf_op jit(solution)/shard_map/whole/pallas_call | solution.py:539
  45.2 1.1 %write.1 = (bf16[512,512]{1,0:T(8,128)(2,1)}, bf16[512,512]{1,0:T(8,128)(2,1)}, bf16[512,128]{1,0:T(8,128)(2,1)}, f32[1,32,256]{2,1,0:T(8,128)}) custom-call(bf16[512,512]{1,0:T(8,128)(2,1)S(1)} %get-tuple-element.8.refs_0_, bf16[512,512]{1,0:T(8,128)(2,1)S(1)} %get-tuple-element.9.refs_1_, bf16[512,128]{1,0:T(8,128)(2,1)S(1)} %get-tuple-element.10.refs_2_, ...), custom_call_target="tpu_custom_call" | custom-call | tf_op jit(solution)/shard_map/write/pallas_call | solution.py:591
